TPU v7x, 32 devices: a whole 2x2x4 slice. The times are simulated.
32 devices in a mesh: fsdp: 8 (over z, y), ctx: 2 (over x), tp: 2 (over core).
Axes of the slice: x: 2, y: 2, z: 4, core: 2. Of those that a mesh axis runs over, the one named last changes fastest.
Arguments:
- tokens: bfloat16 [8, 2, 1280, 768], P('fsdp', 'ctx'), may hold values from -6 to 6
- cotangent: bfloat16 [8, 2, 1280, 768], P('fsdp', 'ctx'), may hold values from -6 to 6
- routes: int32 [8, 2, 1280, 1], P('fsdp', 'ctx', 'tp'), may hold values from 0 to 15; in each aligned block of 640 rows (0 to 639, 640 to 1279, ..., all dimensions but the last counted through in order) at most 80 rows name the same one
- qkv_weight: bfloat16 [3, 768, 768], P(None, 'fsdp', 'tp'), may hold values from -0.3125 to 0.3125
- out_weight: bfloat16 [768, 768], P('tp', 'fsdp'), may hold values from -0.625 to 0.625
- layer_norm_gains: float32 [2, 768], replicated, may hold values from 0.5 to 1.5
- layer_norm_biases: float32 [2, 768], replicated, may hold values from -2 to 2
- up_weight: bfloat16 [16, 768, 3072], P('fsdp', ('ctx', 'tp')), may hold values from -0.21875 to 0.21875
- up_shift: bfloat16 [16, 3072], P('fsdp', ('ctx', 'tp')), may hold values from -2 to 2
- down_weight: bfloat16 [16, 3072, 768], P('fsdp', ('ctx', 'tp')), may hold values from -0.3125 to 0.3125
- down_shift: bfloat16 [16, 768], P('fsdp', ('ctx', 'tp')), may hold values from -2 to 2
- centroids: bfloat16 [16, 768], P('fsdp', ('ctx', 'tp')), may hold values from -0.15625 to 0.15625
Outputs:
- mixed: bfloat16 [8, 2, 1280, 768], P('fsdp', 'ctx')
- tokens_grad: float32 [8, 2, 1280, 768], P('fsdp', 'ctx')
- qkv_grad: float32 [3, 768, 768], P(None, ('fsdp', 'ctx'), 'tp')
- out_grad: float32 [768, 768], P('tp', ('fsdp', 'ctx'))
- gains_grad: float32 [2, 768], P(None, ('fsdp', 'ctx'))
- shifts_grad: float32 [2, 768], P(None, ('fsdp', 'ctx'))
- up_grad: float32 [16, 768, 3072], P('fsdp', ('ctx', 'tp'))
- up_shift_grad: float32 [16, 3072], P('fsdp', ('ctx', 'tp'))
- down_grad: float32 [16, 3072, 768], P('fsdp', ('ctx', 'tp'))
- down_shift_grad: float32 [16, 768], P('fsdp', ('ctx', 'tp'))
- centroids_grad: float32 [16, 768], P('fsdp', ('ctx', 'tp'))
Inputs may be any that keep to these rules, and one draw needn't show every extreme that they name: `routes`: in each aligned block of 640 tokens (the tokens of dimension 2 taken in halves of a block, in order), no expert is named more than 80 times, a bound that some block reaches.
All inputs are finite; a program needn't handle non-finite values.
Results may differ from a plain program's by a relative error of at most 0.024.
Values may be sent and summed in bfloat16 or wider, within the bound.
No kernel may reach another device: no remote copies, remote signals or barrier semaphores. Data moves between devices by JAX's collectives and lax.ppermute only.
A program may use at most 256 MiB of HBM per device.

v0:
```python
from functools import partial
import jax
import jax.numpy as jnp
from jax import lax
from jax.sharding import PartitionSpec as P

HEAD_DIM = 64
PROMPT = 2048
LEN = 256
EPS = 1e-05
NEG = -1e30


def norm_input_rows(values, gain, shift):
    mean = jnp.mean(values, axis=-1, keepdims=True)
    centred = values - mean
    spread = lax.rsqrt(jnp.mean(centred * centred, axis=-1, keepdims=True) + EPS)
    normed = centred * spread
    return (normed * gain + shift, normed, spread)


def norm_back(upstream, normed, spread, gain):
    scaled = upstream * gain
    inner = (
        scaled
        - jnp.mean(scaled, axis=-1, keepdims=True)
        - normed * jnp.mean(scaled * normed, axis=-1, keepdims=True)
    )
    return (spread * inner, jnp.sum(upstream * normed, axis=0), jnp.sum(upstream, axis=0))


def allowed_keys(place, pslice, prompt, length):
    shape = (pslice + length, prompt + length)
    rows = lax.broadcasted_iota(jnp.int32, shape, 0)
    cols = lax.broadcasted_iota(jnp.int32, shape, 1)
    prompt_row = rows < pslice
    prompt_col = cols < prompt
    early = prompt_row & prompt_col & (cols <= place * pslice + rows)
    later = jnp.logical_not(prompt_row) & (prompt_col | (cols - prompt <= rows - pslice))
    return early | later


def dense_weights(qkv_weight, out_weight):
    return (
        lax.all_gather(qkv_weight, "fsdp", axis=1, tiled=True),
        lax.all_gather(out_weight, "fsdp", axis=1, tiled=True),
    )


def expert_weights(up_weight, down_weight, up_shift, down_shift, centroids):
    return (
        lax.all_gather(up_weight, ("ctx", "tp"), axis=1, tiled=True),
        lax.all_gather(down_weight, ("ctx", "tp"), axis=1, tiled=True),
        lax.all_gather(up_shift, ("ctx", "tp"), axis=1, tiled=True),
        lax.all_gather(down_shift, ("ctx", "tp"), axis=1, tiled=True),
        lax.all_gather(centroids, ("ctx", "tp"), axis=1, tiled=True),
    )


def tp_rows(rows):
    return lax.all_gather(rows, "tp", axis=0, tiled=True)


def head_total(terms):
    return lax.psum(terms.astype(jnp.bfloat16), "tp").astype(jnp.float32)


def split_heads(matrix):
    return matrix.reshape(matrix.shape[0], -1, HEAD_DIM).transpose(1, 0, 2)


def join_heads(stacked):
    return stacked.transpose(1, 0, 2).reshape(stacked.shape[1], -1)


def head_forward(allowed, scale, parts):
    query, keys, values = parts
    raw = jnp.einsum("qd,kd->qk", query, keys, preferred_element_type=jnp.float32) * scale
    scores = jnp.where(allowed, raw, NEG)
    top = jnp.max(scores, axis=-1, keepdims=True)
    weights = jnp.exp(scores - top)
    total = jnp.sum(weights, axis=-1, keepdims=True)
    shares = (weights / total).astype(jnp.bfloat16)
    context = jnp.dot(shares, values, preferred_element_type=jnp.float32).astype(jnp.bfloat16)
    return (context, (top + jnp.log(total))[:, 0])


def head_backward(allowed, scale, parts):
    query, keys, values, context_grad, log_total = parts
    raw = jnp.einsum("qd,kd->qk", query, keys, preferred_element_type=jnp.float32) * scale
    scores = jnp.where(allowed, raw, NEG)
    weights = jnp.exp(scores - log_total[:, None])
    values_grad = jnp.einsum(
        "qk,qd->kd", weights.astype(jnp.bfloat16), context_grad, preferred_element_type=jnp.float32
    )
    weight_grad = jnp.einsum("qd,kd->qk", context_grad, values, preferred_element_type=jnp.float32)
    row_dot = jnp.sum(weights * weight_grad, axis=-1, keepdims=True)
    logit_grad = (weights * (weight_grad - row_dot)).astype(jnp.bfloat16)
    query_grad = jnp.dot(logit_grad, keys, preferred_element_type=jnp.float32) * scale
    keys_grad = (
        jnp.einsum("qk,qd->kd", logit_grad, query, preferred_element_type=jnp.float32) * scale
    )
    return (query_grad, keys_grad, values_grad)


def shards(
    tokens,
    cotangent,
    routes,
    qkv_weight,
    out_weight,
    layer_norm_gains,
    layer_norm_biases,
    up_weight,
    up_shift,
    down_weight,
    down_shift,
    centroids,
):
    block = tokens.shape[2]
    width = tokens.shape[3]
    pslice = block - LEN
    half = routes.shape[2]
    place = lax.axis_index("ctx")
    half_start = lax.axis_index("tp") * half
    scale = HEAD_DIM ** (-0.5)
    residual_stream = tokens.reshape(block, width).astype(jnp.float32)
    project_full, output_full = dense_weights(qkv_weight, out_weight)
    first_normed_rows, first_standardized, first_deviation = norm_input_rows(
        residual_stream, layer_norm_gains[0], layer_norm_biases[0]
    )
    first = first_normed_rows.astype(jnp.bfloat16)
    projected = jnp.einsum(
        "rd,jde->jre", first, project_full, preferred_element_type=jnp.float32
    ).astype(jnp.bfloat16)
    queries, keys_own, values_own = (projected[0], projected[1], projected[2])
    prompt_keys, prompt_values = (
        lax.all_gather(keys_own[:pslice], "ctx", axis=0, tiled=True),
        lax.all_gather(values_own[:pslice], "ctx", axis=0, tiled=True),
    )
    keys_all = jnp.concatenate([prompt_keys, keys_own[pslice:]], axis=0)
    values_all = jnp.concatenate([prompt_values, values_own[pslice:]], axis=0)
    allowed = allowed_keys(place, pslice, PROMPT, LEN)
    query_heads = split_heads(queries)
    key_heads = split_heads(keys_all)
    value_heads = split_heads(values_all)
    context_heads, log_total = lax.map(
        partial(head_forward, allowed, scale), (query_heads, key_heads, value_heads)
    )
    context = join_heads(context_heads)
    attended = head_total(jnp.dot(context, output_full, preferred_element_type=jnp.float32))
    residual_rows = residual_stream + attended
    second_normed_rows, second_standardized, second_deviation = norm_input_rows(
        residual_rows, layer_norm_gains[1], layer_norm_biases[1]
    )
    second = second_normed_rows.astype(jnp.bfloat16)
    own_rows = lax.dynamic_slice_in_dim(second, half_start, half, 0)
    route = routes.reshape(half)
    local_experts = up_weight.shape[0]
    owners = lax.axis_size("fsdp")
    total_experts = local_experts * owners
    capacity = 2 * half // total_experts
    slots = total_experts * capacity
    member = (route[:, None] == lax.broadcasted_iota(jnp.int32, (half, total_experts), 1)).astype(
        jnp.int32
    )
    rank = jnp.sum((jnp.cumsum(member, axis=0) - 1) * member, axis=1)
    slot_of = route * capacity + rank
    placing = (lax.broadcasted_iota(jnp.int32, (slots, half), 0) == slot_of[None, :]).astype(
        jnp.bfloat16
    )
    outgoing = (
        jnp.dot(placing, own_rows, preferred_element_type=jnp.float32)
        .astype(jnp.bfloat16)
        .reshape(owners, local_experts, capacity, width)
    )
    up_full, down_full, up_bias, down_bias, centres = expert_weights(
        up_weight, down_weight, up_shift, down_shift, centroids
    )
    arrived = lax.all_to_all(outgoing, "fsdp", split_axis=0, concat_axis=0, tiled=True)
    score = jnp.einsum("sekd,ed->sek", arrived, centres, preferred_element_type=jnp.float32)
    gate = jax.nn.sigmoid(score)
    inner = jnp.einsum(
        "sekd,edf->sekf", arrived, up_full, preferred_element_type=jnp.float32
    ) + up_bias[None, :, None, :].astype(jnp.float32)
    hidden = jax.nn.gelu(inner, approximate=False).astype(jnp.bfloat16)
    result = jnp.einsum(
        "sekf,efd->sekd", hidden, down_full, preferred_element_type=jnp.float32
    ) + down_bias[None, :, None, :].astype(jnp.float32)
    sent = (gate[..., None] * result).astype(jnp.bfloat16)
    returned = lax.all_to_all(sent, "fsdp", split_axis=0, concat_axis=0, tiled=True)
    returned, arrived, inner, hidden, gate, result = (
        returned,
        arrived,
        inner,
        hidden,
        gate,
        result,
    )
    back_rows = jnp.einsum(
        "sr,sd->rd", placing, returned.reshape(slots, width), preferred_element_type=jnp.float32
    ).astype(jnp.bfloat16)
    expert_out = tp_rows(back_rows)
    mixed = (residual_rows + expert_out.astype(jnp.float32)).astype(jnp.bfloat16)
    project_back, output_back = dense_weights(qkv_weight, out_weight)
    up_back, down_back, unused_up, unused_down, centre_back = expert_weights(
        up_weight, down_weight, up_shift, down_shift, centroids
    )
    upstream_rows = cotangent.reshape(block, width)
    upstream = upstream_rows.astype(jnp.float32)
    upstream_half = lax.dynamic_slice_in_dim(upstream_rows, half_start, half, 0)
    grad_out = (
        jnp.dot(placing, upstream_half, preferred_element_type=jnp.float32)
        .astype(jnp.bfloat16)
        .reshape(owners, local_experts, capacity, width)
    )
    arrived_grad = lax.all_to_all(grad_out, "fsdp", split_axis=0, concat_axis=0, tiled=True).astype(
        jnp.float32
    )
    result_grad = (gate[..., None] * arrived_grad).astype(jnp.bfloat16)
    gate_grad = jnp.sum(arrived_grad * result, axis=-1)
    score_grad = (gate_grad * gate * (1.0 - gate)).astype(jnp.bfloat16)
    hidden_grad = jnp.einsum(
        "sekd,efd->sekf", result_grad, down_back, preferred_element_type=jnp.float32
    )
    gelu_pull = jax.vjp(partial(jax.nn.gelu, approximate=False), inner)[1]
    inner_grad = gelu_pull(hidden_grad)[0].astype(jnp.bfloat16)
    rows_grad = jnp.einsum(
        "sekf,edf->sekd", inner_grad, up_back, preferred_element_type=jnp.float32
    )
    rows_grad = rows_grad + score_grad.astype(jnp.float32)[..., None] * centre_back[
        None, :, None, :
    ].astype(jnp.float32)
    sent_grad = lax.all_to_all(
        rows_grad.astype(jnp.bfloat16), "fsdp", split_axis=0, concat_axis=0, tiled=True
    )
    up_local = jnp.einsum("sekd,sekf->edf", arrived, inner_grad, preferred_element_type=jnp.float32)
    down_local = jnp.einsum(
        "sekf,sekd->efd", hidden, result_grad, preferred_element_type=jnp.float32
    )
    up_shift_local = jnp.sum(inner_grad.astype(jnp.float32), axis=(0, 2))
    down_shift_local = jnp.sum(result_grad.astype(jnp.float32), axis=(0, 2))
    centre_local = jnp.einsum(
        "sek,sekd->ed", score_grad, arrived, preferred_element_type=jnp.float32
    )
    up_grad, down_grad, up_shift_grad, down_shift_grad, centroids_grad = (
        lax.psum_scatter(
            up_local.astype(jnp.bfloat16), ("ctx", "tp"), scatter_dimension=1, tiled=True
        ).astype(jnp.float32),
        lax.psum_scatter(
            down_local.astype(jnp.bfloat16), ("ctx", "tp"), scatter_dimension=1, tiled=True
        ).astype(jnp.float32),
        lax.psum_scatter(
            up_shift_local.astype(jnp.bfloat16), ("ctx", "tp"), scatter_dimension=1, tiled=True
        ).astype(jnp.float32),
        lax.psum_scatter(
            down_shift_local.astype(jnp.bfloat16), ("ctx", "tp"), scatter_dimension=1, tiled=True
        ).astype(jnp.float32),
        lax.psum_scatter(
            centre_local.astype(jnp.bfloat16), ("ctx", "tp"), scatter_dimension=1, tiled=True
        ).astype(jnp.float32),
    )
    half_grad = jnp.einsum(
        "sr,sd->rd", placing, sent_grad.reshape(slots, width), preferred_element_type=jnp.float32
    ).astype(jnp.bfloat16)
    second_norm_gradient = tp_rows(half_grad).astype(jnp.float32)
    resid_norm_grad, gain_two_grad, shift_two_grad = norm_back(
        second_norm_gradient, second_standardized, second_deviation, layer_norm_gains[1]
    )
    resid_grad = upstream + resid_norm_grad
    attended_grad = resid_grad.astype(jnp.bfloat16)
    output_grad = jnp.einsum(
        "rh,rd->hd", context, attended_grad, preferred_element_type=jnp.float32
    )
    context_grad = jnp.einsum(
        "rd,hd->rh", attended_grad, output_back, preferred_element_type=jnp.float32
    ).astype(jnp.bfloat16)
    query_grad, keys_grad, values_grad = lax.map(
        partial(head_backward, allowed, scale),
        (query_heads, key_heads, value_heads, split_heads(context_grad), log_total),
    )
    keys_flat = join_heads(keys_grad)
    values_flat = join_heads(values_grad)
    prompt_key_grad, prompt_value_grad = (
        lax.psum_scatter(
            keys_flat[:PROMPT].astype(jnp.bfloat16), "ctx", scatter_dimension=0, tiled=True
        ).astype(jnp.float32),
        lax.psum_scatter(
            values_flat[:PROMPT].astype(jnp.bfloat16), "ctx", scatter_dimension=0, tiled=True
        ).astype(jnp.float32),
    )
    keys_total = jnp.concatenate([prompt_key_grad, keys_flat[PROMPT:]], axis=0).astype(jnp.bfloat16)
    values_total = jnp.concatenate([prompt_value_grad, values_flat[PROMPT:]], axis=0).astype(
        jnp.bfloat16
    )
    queries_total = join_heads(query_grad).astype(jnp.bfloat16)
    stacked = jnp.stack([queries_total, keys_total, values_total])
    project_grad = jnp.einsum("rd,jre->jde", first, stacked, preferred_element_type=jnp.float32)
    first_norm_gradient = head_total(
        jnp.einsum("jre,jde->rd", stacked, project_back, preferred_element_type=jnp.float32)
    )
    stream_norm_grad, gain_one_grad, shift_one_grad = norm_back(
        first_norm_gradient, first_standardized, first_deviation, layer_norm_gains[0]
    )
    tokens_grad = resid_grad + stream_norm_grad
    gains_local = jnp.stack([gain_one_grad, gain_two_grad])
    shifts_local = jnp.stack([shift_one_grad, shift_two_grad])
    qkv_grad, out_grad, gains_grad, shifts_grad = (
        lax.psum_scatter(project_grad, ("fsdp", "ctx"), scatter_dimension=1, tiled=True),
        lax.psum_scatter(output_grad, ("fsdp", "ctx"), scatter_dimension=1, tiled=True),
        lax.psum_scatter(gains_local, ("fsdp", "ctx"), scatter_dimension=1, tiled=True),
        lax.psum_scatter(shifts_local, ("fsdp", "ctx"), scatter_dimension=1, tiled=True),
    )
    return (
        mixed.reshape(1, 1, block, width),
        tokens_grad.reshape(1, 1, block, width),
        qkv_grad,
        out_grad,
        gains_grad,
        shifts_grad,
        up_grad,
        up_shift_grad,
        down_grad,
        down_shift_grad,
        centroids_grad,
    )


def solution(mesh):
    in_specs = (
        P("fsdp", "ctx", None, None),
        P("fsdp", "ctx", None, None),
        P("fsdp", "ctx", "tp", None),
        P(None, "fsdp", "tp"),
        P("tp", "fsdp"),
        P(),
        P(),
        P("fsdp", ("ctx", "tp"), None),
        P("fsdp", ("ctx", "tp")),
        P("fsdp", ("ctx", "tp"), None),
        P("fsdp", ("ctx", "tp")),
        P("fsdp", ("ctx", "tp")),
    )
    out_specs = (
        P("fsdp", "ctx", None, None),
        P("fsdp", "ctx", None, None),
        P(None, ("fsdp", "ctx"), "tp"),
        P("tp", ("fsdp", "ctx")),
        P(None, ("fsdp", "ctx")),
        P(None, ("fsdp", "ctx")),
        P("fsdp", ("ctx", "tp"), None),
        P("fsdp", ("ctx", "tp")),
        P("fsdp", ("ctx", "tp"), None),
        P("fsdp", ("ctx", "tp")),
        P("fsdp", ("ctx", "tp")),
    )
    return jax.shard_map(shards, mesh=mesh, in_specs=in_specs, out_specs=out_specs, check_vma=False)
```

profile of v0, /device:TPU:0, one launch (start us, length us, event | category | flops | bytes accessed | tf_op | source)
XLA Modules:
  0.0 1489.0 jit_solution(16068740951477841922)
XLA Ops:
  14.4 45.3 %all-gather.12.cloned.1.call-done = bf16[3,768,384]{2,1,0:T(8,128)(2,1)} async-done(((bf16[3,96,384]{2,1,0:T(8,128)(2,1)}), bf16[3,768,384]{2,1,0:T(8,128)(2,1)}) %all-gather.12.cloned.1.call-update) | async-done | bytes 1769488 | tf_op jit(solution)/shard_map/all_gather | solution.py:45
  70.2 34.0 %all_gather.41 = bf16[384,768]{0,1:T(8,128)(2,1)} all-gather(bf16[384,96]{0,1:T(8,128)(2,1)S(1)} %copy-done.25), channel_id=1, replica_groups=mesh['fsdp'=8,'ctx'=2,'tp'=2] {'fsdp'}, dimensions={1}, use_global_device_ids=true | all-gather | bytes 663552 | tf_op jit(solution)/shard_map/all_gather | solution.py:46
  111.3 11.0 all-gather.24.cloned.1.call-done
  130.0 82.3 %while.28 = (s32[]{:T(128)}, bf16[6,1280,64]{1,2,0:T(8,128)(2,1)}, f32[6,1280]{1,0:T(8,128)}, bf16[6,1280,64]{2,1,0:T(8,128)(2,1)}, bf16[6,2304,64]{2,1,0:T(8,12...) while((s32[]{:T(128)}, bf16[6,1280,64]{1,2,0:T(8,128)(2,1)}, ...), condition=%wide.region_5.6_spmd.clone, body=%wide.region_2.5_spmd.clone.sunk | while | flops 799292160 | bytes 37163152 | solution.py:147
  130.0 6.9 fusion.199
  143.7 6.9 fusion.199
  221.1 18.6 %all-reduce.5.cloned.1.call-done = bf16[1280,768]{1,0:T(8,128)(2,1)} async-done(((bf16[1280,768]{1,0:T(8,128)(2,1)}), bf16[1280,768]{1,0:T(8,128)(2,1)}) %all-reduce.5.cloned.1.call-update) | async-done | bytes 1966096 | tf_op jit(solution)/shard_map/psum | solution.py:65
  273.9 26.3 %all-to-all-done = bf16[8,2,80,768]{3,2,1,0:T(8,128)(2,1)} async-done(((bf16[8,2,80,768]{3,2,1,0:T(8,128)(2,1)}), bf16[8,2,80,768]{3,2,1,0:T(8,128)(2,1)}, u32[]{:S(2)}, u32[]{:S(2)}) %all-to-all-start) | async-done | bytes 1966112 | tf_op jit(solution)/shard_map/all_to_all | solution.py:180
  306.3 43.6 %fusion.66 = (bf16[8,2,80,3072]{3,2,0,1:T(8,128)(2,1)}, f32[8,2,80,3072]{3,2,0,1:T(8,128)}, f32[2,8,80,3072]{3,2,1,0:T(8,128)}) fusion(f32[2,3072]{1,0:T(2,128)S(1)} %convert_element_type.197, bf16[2,768,3072]{2,1,0:T(8,128)(2,1)} %all-gather.14.cloned.1.call-done, bf16[8,2,80,768]{3,2,1,0:T(8,128)(2,1)} %all-to-all-done), kind=kOutput, calls=%fused_computation.82 | convolution fusion | flops 6299320320 | bytes 50749440 | tf_op jit(solution)/shard_map/sekd,edf->sekf/dot_general | solution.py:183
  349.9 13.3 fusion.110
  363.8 23.0 %fusion.167 = (bf16[2,3072]{1,0:T(2,128)(2,1)}, bf16[8,2,80,3072]{3,2,0,1:T(8,128)(2,1)}) fusion(f32[8,2,80,3072]{3,2,0,1:T(8,128)} %get-tuple-element.291, bf16[2,3072,768]{2,1,0:T(8,128)(2,1)} %all-gather.16.cloned.1.call-done, f32[8,2,80]{2,0,1:T(8,128)S(1)} %divide_bitcast_fusion, bf16[8,2,80,768]{3,2,1,0:T(8,128)(2,1)S(1)} %all-to-all-done.2, ...), kind=kOutput, calls=%fused_computation.234 | convolution fusion | flops 6105655296 | bytes 50766848 | tf_op jit(solution)/shard_map/sekd,efd->sekf/dot_general | solution.py:223
  386.8 11.4 fusion.118
  398.4 51.3 %all_to_all.20 = bf16[8,2,80,768]{3,2,1,0:T(8,128)(2,1)S(1)} all-to-all(bf16[8,2,80,768]{3,2,1,0:T(8,128)(2,1)S(1)} %copy.90), channel_id=1, replica_groups=mesh['fsdp'=8,'ctx'=2,'tp'=2] {'fsdp'}, dimensions={0} | all-to-all | bytes 3932160 | tf_op jit(solution)/shard_map/all_to_all | solution.py:234
  452.4 9.1 all-gather.20.cloned.1.call-done
  475.3 139.5 %while.29 = (s32[]{:T(128)}, bf16[6,1280,64]{1,2,0:T(8,128)(2,1)}, bf16[6,2304,64]{1,2,0:T(8,128)(2,1)}, bf16[6,2304,64]{1,2,0:T(8,128)(2,1)}, bf16[6,1280,64]{2...) while((s32[]{:T(128)}, bf16[6,1280,64]{1,2,0:T(8,128)(2,1)}, ...), condition=%wide.region_17.18_spmd.clone, body=%wide.region_15.17_spmd.clone.sunk | while | flops 1934850816 | bytes 107280608 | solution.py:278
  479.0 8.8 multiply_reduce_fusion.3
  502.2 8.8 multiply_reduce_fusion.3
  525.4 8.8 multiply_reduce_fusion.3
  548.6 8.8 multiply_reduce_fusion.3
  571.8 8.8 multiply_reduce_fusion.3
  594.9 8.8 multiply_reduce_fusion.3
  631.3 14.0 reduce-scatter.23.cloned.1.call-done
  645.3 29.0 %reduce-scatter.21.cloned.1.call-done = bf16[1024,384]{1,0:T(8,128)(2,1)} async-done(((bf16[2048,384]{1,0:T(8,128)(2,1)}), bf16[1024,384]{1,0:T(8,128)(2,1)}) %reduce-scatter.21.cloned.1.call-update) | async-done | bytes 786448 | tf_op jit(solution)/shard_map/reduce_scatter | solution.py:285
  690.8 10.9 all-reduce.7.cloned.1.call-done
  719.4 13.2 bitcast_convert_fusion.1
  732.6 13.2 bitcast_convert_fusion
  763.7 117.0 %reduce-scatter.31.cloned.1.call-done = f32[48,2]{1,0:T(8,128)} async-done(((f32[768,2]{1,0:T(8,128)}), f32[48,2]{1,0:T(8,128)}) %reduce-scatter.31.cloned.1.call-update) | async-done | bytes 400
  882.0 125.4 %reduce-scatter.33.cloned.1.call-done = f32[48,2]{1,0:T(8,128)} async-done(((f32[768,2]{1,0:T(8,128)}), f32[48,2]{1,0:T(8,128)}) %reduce-scatter.33.cloned.1.call-update) | async-done | bytes 400
  1008.8 182.4 %all-reduce.9.cloned.1.call-done = f32[3,768,384]{2,0,1:T(4,128)} async-done(((f32[3,768,384]{2,0,1:T(4,128)}), f32[3,768,384]{2,0,1:T(4,128)}) %all-reduce.9.cloned.1.call-update) | async-done | bytes 3538960
  1192.9 77.6 %reduce-scatter.27.cloned.1.call-done = bf16[2,192,3072]{2,1,0:T(8,128)(2,1)} async-done(((bf16[2,768,3072]{2,1,0:T(8,128)(2,1)}), bf16[2,192,3072]{2,1,0:T(8,128)(2,1)}) %reduce-scatter.27.cloned.1.call-update) | async-done | bytes 2359312 | tf_op jit(solution)/shard_map/reduce_scatter | solution.py:247
  1275.0 76.0 %reduce-scatter.29.cloned.1.call-done = bf16[2,768,768]{2,1,0:T(8,128)(2,1)} async-done(((bf16[2,3072,768]{2,1,0:T(8,128)(2,1)}), bf16[2,768,768]{2,1,0:T(8,128)(2,1)}) %reduce-scatter.29.cloned.1.call-update) | async-done | bytes 2359312 | tf_op jit(solution)/shard_map/reduce_scatter | solution.py:250
  1355.2 126.0 %reduce-scatter.25.cloned.1.call-done = f32[384,48]{0,1:T(8,128)} async-done(((f32[384,768]{0,1:T(8,128)}), f32[384,48]{0,1:T(8,128)}) %reduce-scatter.25.cloned.1.call-update) | async-done | bytes 73744 | tf_op jit(solution)/shard_map/reduce_scatter | solution.py:310
  (353 shorter events, 332.2 us)
Async XLA Ops:
  8.0 51.7 %copy-start = (bf16[1,1,1280,768]{3,2,1,0:T(8,128)(2,1)S(1)}, bf16[1,1,1280,768]{3,2,1,0:T(8,128)(2,1)}, u32[]{:S(2)}) copy-start(bf16[1,1,1280,768]{3,2,1,0:T(8,128)(2,1)} %param.16) | copy-start | bytes 5898244
  8.0 51.7 %all-gather.12.cloned.1.call-start = ((), (), s32[]{:S(2)}) async-start(), calls=%async_computation.14 | async-start | bytes 1990656 | tf_op jit(solution)/shard_map/all_gather | solution.py:45
  8.8 99.5 %all-gather.22.cloned.1.call-start = ((), (), s32[]{:S(2)}) async-start(), calls=%async_computation.26 | async-start | bytes 2359296 | tf_op jit(solution)/shard_map/all_gather | solution.py:138
  10.2 53.8 %copy-start.28 = (f32[768]{0:T(1024)}, f32[768]{0:T(1024)S(1)}, u32[]{:S(2)}) copy-start(f32[768]{0:T(1024)S(1)} %get-tuple-element.307) | copy-start | bytes 9220
  10.2 53.8 %copy-start.40 = (f32[768]{0:T(1024)}, f32[768]{0:T(1024)S(1)}, u32[]{:S(2)}) copy-start(f32[768]{0:T(1024)S(1)} %get-tuple-element.233) | copy-start | bytes 9220
  12.1 52.0 %copy-start.21 = (f32[1280]{0:T(1024)}, f32[1280]{0:T(1024)S(1)}, u32[]{:S(2)}) copy-start(f32[1280]{0:T(1024)S(1)} %broadcast_multiply_fusion.5) | copy-start | bytes 15364
  14.4 49.7 %copy-start.23 = (f32[1280]{0:T(1024)}, f32[1280]{0:T(1024)S(1)}, u32[]{:S(2)}) copy-start(f32[1280]{0:T(1024)S(1)} %add_rsqrt_fusion.1) | copy-start | bytes 15364
  67.0 37.2 %slice-start = ((bf16[3,1280,384]{1,2,0:T(8,128)(2,1)}), bf16[1,1280,384]{1,2,0:T(8,128)(2,1)S(1)}, s32[]{:S(2)}) async-start(bf16[3,1280,384]{1,2,0:T(8,128)(2,1)} %copy-done.11), calls=%async_computation.34 | async-start | bytes 1966080 | tf_op jit(solution)/shard_map/slice | solution.py:136
  67.1 55.3 %all-gather.24.cloned.1.call-start = ((), (), s32[]{:S(2)}) async-start(), calls=%async_computation.27 | async-start | bytes 2359296 | tf_op jit(solution)/shard_map/all_gather | solution.py:139
  67.8 171.8 %all-reduce.5.cloned.1.call-start = ((), (), s32[]{:S(2)}) async-start(), calls=%async_computation.15 | async-start | bytes 3932160 | tf_op jit(solution)/shard_map/psum | solution.py:65
  218.0 88.3 %all-gather.14.cloned.1.call-start = ((), (), s32[]{:S(2)}) async-start(), calls=%async_computation.16 | async-start | bytes 11796480 | tf_op jit(solution)/shard_map/all_gather | solution.py:52
  218.6 131.3 %all-gather.16.cloned.1.call-start = ((), (), s32[]{:S(2)}) async-start(), calls=%async_computation.17 | async-start | bytes 11796480 | tf_op jit(solution)/shard_map/all_gather | solution.py:53
  221.1 49.8 %copy-start.42 = (s32[640]{0:T(1024)}, s32[640]{0:T(1024)S(1)}, u32[]{:S(2)}) copy-start(s32[640]{0:T(1024)S(1)} %multiply_add_fusion) | copy-start | bytes 7684
  248.6 51.6 %all-to-all-start = ((bf16[8,2,80,768]{3,2,1,0:T(8,128)(2,1)}), bf16[8,2,80,768]{3,2,1,0:T(8,128)(2,1)}, u32[]{:S(2)}, u32[]{:S(2)}) async-start(bf16[8,2,80,768]{3,2,1,0:T(8,128)(2,1)} %bitcast.381), calls=%async_computation | async-start | bytes 3932160 | tf_op jit(solution)/shard_map/all_to_all | solution.py:180
  300.2 49.7 %all-to-all-start.2 = ((bf16[8,2,80,768]{3,2,1,0:T(8,128)(2,1)}), bf16[8,2,80,768]{3,2,1,0:T(8,128)(2,1)S(1)}, u32[]{:S(2)}, u32[]{:S(2)}) async-start(bf16[8,2,80,768]{3,2,1,0:T(8,128)(2,1)} %bitcast.380), calls=%async_computation.2 | async-start | bytes 3932160 | tf_op jit(solution)/shard_map/all_to_all | solution.py:217
  303.9 157.7 %all-gather.20.cloned.1.call-start = ((), (), s32[]{:S(2)}) async-start(), calls=%async_computation.19 | async-start | bytes 2949120 | tf_op jit(solution)/shard_map/all_gather | solution.py:61
  306.2 57.6 %copy-start.32 = (f32[8,2,80]{2,0,1:T(8,128)}, f32[8,2,80]{2,0,1:T(8,128)S(1)}, u32[]{:S(2)}) copy-start(f32[8,2,80]{2,0,1:T(8,128)S(1)} %divide_bitcast_fusion) | copy-start | bytes 15364
  398.2 51.4 %copy-start.43 = (s32[640]{0:T(1024)S(1)}, s32[640]{0:T(1024)}, u32[]{:S(2)}) copy-start(s32[640]{0:T(1024)} %copy-done.42) | copy-start | bytes 7684
  452.4 192.9 %reduce-scatter.23.cloned.1.call-start = ((), (), s32[]{:S(2)}) async-start(), calls=%async_computation.21 | async-start | bytes 2359296 | tf_op jit(solution)/shard_map/reduce_scatter | solution.py:288
  617.8 56.5 %reduce-scatter.21.cloned.1.call-start = ((), (), s32[]{:S(2)}) async-start(), calls=%async_computation.20 | async-start | bytes 2359296 | tf_op jit(solution)/shard_map/reduce_scatter | solution.py:285
  622.6 63.6 %all-to-all-start.1 = ((bf16[8,2,80,768]{3,2,1,0:T(8,128)(2,1)}), bf16[8,2,80,768]{3,2,1,0:T(8,128)(2,1)}, u32[]{:S(2)}, u32[]{:S(2)}) async-start(bf16[8,2,80,768]{3,2,1,0:T(8,128)(2,1)} %copy.88), calls=%async_computation.1 | async-start | bytes 3932160 | tf_op jit(solution)/shard_map/all_to_all | solution.py:191
  628.4 73.3 %all-reduce.7.cloned.1.call-start = ((), (), s32[]{:S(2)}) async-start(), calls=%async_computation.22 | async-start | bytes 3932160 | tf_op jit(solution)/shard_map/psum | solution.py:65
  680.5 72.2 %reduce-scatter.37.cloned.1.call-start = ((), (), s32[]{:S(2)}) async-start(), calls=%async_computation.31 | async-start | bytes 245760
  681.9 72.3 %reduce-scatter.39.cloned.1.call-start = ((), (), s32[]{:S(2)}) async-start(), calls=%async_computation.32 | async-start | bytes 245760
  684.8 70.8 %reduce-scatter.35.cloned.1.call-start = ((), (), s32[]{:S(2)}) async-start(), calls=%async_computation.30 | async-start | bytes 983040
  686.2 71.2 %all-gather.18.cloned.1.call-start = ((), (), s32[]{:S(2)}) async-start(), calls=%async_computation.18 | async-start | bytes 2949120 | tf_op jit(solution)/shard_map/all_gather | solution.py:61
  690.7 190.0 %reduce-scatter.31.cloned.1.call-start = ((), (), s32[]{:S(2)}) async-start(), calls=%async_computation.28 | async-start | bytes 417792
  706.1 301.4 %reduce-scatter.33.cloned.1.call-start = ((), (), s32[]{:S(2)}) async-start(), calls=%async_computation.29 | async-start | bytes 417792
  707.1 484.1 %all-reduce.9.cloned.1.call-start = ((), (), s32[]{:S(2)}) async-start(), calls=%async_computation.33 | async-start | bytes 9437184
  719.3 551.2 %reduce-scatter.27.cloned.1.call-start = ((), (), s32[]{:S(2)}) async-start(), calls=%async_computation.24 | async-start | bytes 11796480 | tf_op jit(solution)/shard_map/reduce_scatter | solution.py:247
  732.6 618.4 %reduce-scatter.29.cloned.1.call-start = ((), (), s32[]{:S(2)}) async-start(), calls=%async_computation.25 | async-start | bytes 11796480 | tf_op jit(solution)/shard_map/reduce_scatter | solution.py:250
  745.9 735.3 %reduce-scatter.25.cloned.1.call-start = ((), (), s32[]{:S(2)}) async-start(), calls=%async_computation.23 | async-start | bytes 1253376 | tf_op jit(solution)/shard_map/reduce_scatter | solution.py:310
  (54 other events, 362.4 us)
Sparse Core Ops, SparseCore 0:
  11.0 48.6 all-gather.11
  67.2 25.7 all-gather.21
  95.1 27.1 all-gather.23
  218.1 21.4 all-reduce.4
  452.5 9.0 all-gather.19
  618.0 27.3 reduce-scatter.22
  648.1 26.1 reduce-scatter.20
  680.6 21.0 all-reduce.6
  703.2 11.5 all-gather.17
Sparse Core Ops, SparseCore 1:
  220.0 64.2 all-gather.13
  285.7 64.1 all-gather.15
  684.0 19.8 reduce-scatter.36
  706.3 20.7 reduce-scatter.38
  729.6 23.1 reduce-scatter.34
  757.4 123.2 reduce-scatter.30
  885.2 122.2 reduce-scatter.32
  1013.6 177.5 all-reduce.8
  1193.7 76.8 reduce-scatter.26
  1273.2 77.8 reduce-scatter.28
  1356.2 124.9 reduce-scatter.24
where the time goes:
time: 1500 us; the launch traced here: 1490 us
  waiting for transfers between devices  871 us (58%)
  matrix products  344 us (23%)
  blocking collectives  101 us (7%)
  local copies, waits for them, and re-layouts  73.5 us (5%)
  other arithmetic  64.7 us (4%)
  between operations  17.5 us (1%)
  starting transfers between devices  16 us (1%)
    unnamed x26, waiting for transfers between devices  427 us
    reduce_scatter x1, waiting for transfers between devices, shards(): lax.psum_scatter(output_grad, ('fsdp', 'ctx'), scatter_dimension=1, tiled...  126 us
    reduce_scatter x1, waiting for transfers between devices, shards(): lax.psum_scatter(up_local.astype(jnp.bfloat16), ('ctx', 'tp'), scatter_di...  77.6 us
    reduce_scatter x1, waiting for transfers between devices, shards(): lax.psum_scatter(down_local.astype(jnp.bfloat16), ('ctx', 'tp'), scatter_...  76 us
    dot_general x6, matrix products, head_backward(): jnp.einsum('qd,kd->qk', query, keys, preferred_element_type=jnp.float32)  53 us
    all_to_all x1, blocking collectives, shards(): lax.all_to_all(rows_grad.astype(jnp.bfloat16), 'fsdp', split_axis=0, conc...  51.3 us
    all_gather x1, waiting for transfers between devices, dense_weights(): lax.all_gather(qkv_weight, 'fsdp', axis=1, tiled=True)  45.3 us
    dot_general x1, matrix products, shards(): jnp.einsum('sekd,edf->sekf', arrived, up_full, preferred_element_type=jnp...  43.6 us
  transfers between devices with their start and end apart: 23, of which 14 were waited for; matrix products, arithmetic and copies ran while one was open for 11% of the time, Pallas kernels for 0%

commit v1 on v0

--- a/solution.py
+++ b/solution.py
@@ -9,6 +9,13 @@
 LEN = 256
 EPS = 1e-05
 NEG = -1e30
+
+
+def arrange_the_array(packet):
+    return jnp.concatenate(
+        lax.all_to_all(jnp.stack([packet for _ in range(lax.axis_size("fsdp"))]), "fsdp", 0, 0),
+        axis=1,
+    )
 
 
 def norm_input_rows(values, gain, shift):
@@ -41,10 +48,7 @@
 
 
 def dense_weights(qkv_weight, out_weight):
-    return (
-        lax.all_gather(qkv_weight, "fsdp", axis=1, tiled=True),
-        lax.all_gather(out_weight, "fsdp", axis=1, tiled=True),
-    )
+    return (lax.all_gather(qkv_weight, "fsdp", axis=1, tiled=True), arrange_the_array(out_weight))
 
 
 def expert_weights(up_weight, down_weight, up_shift, down_shift, centroids):

time: 1500 us -> 1500 us (level)
  blocking collectives: 101 us -> 67 us
  waiting for transfers between devices: 871 us -> 900 us
    all_gather x1 -> x0, blocking collectives: 34 us -> none  [dense_weights(): lax.all_gather(out_weight, 'fsdp', axis=1, tiled=True)]
    all_gather x1, waiting for transfers between devices: 11 us -> 26.3 us  [shards(): lax.all_gather(values_own[:pslice], 'ctx', axis=0, tiled=True)]
  transfers between devices with their start and end apart: 23 -> 24, of which waited for: 14 -> 15; matrix products, arithmetic and copies ran while one was open for 11% -> 17% of each run, Pallas kernels for 0% -> 0%
where the time goes in v1:
time: 1500 us; the launch traced here: 1490 us
  waiting for transfers between devices  900 us (60%)
  matrix products  344 us (23%)
  local copies, waits for them, and re-layouts  74.3 us (5%)
  blocking collectives  67 us (4%)
  other arithmetic  64.7 us (4%)
  starting transfers between devices  20.6 us (1%)
  between operations  17.6 us (1%)
    unnamed x26, waiting for transfers between devices  428 us
    reduce_scatter x1, waiting for transfers between devices, shards(): lax.psum_scatter(output_grad, ('fsdp', 'ctx'), scatter_dimension=1, tiled...  126 us
    reduce_scatter x1, waiting for transfers between devices, shards(): lax.psum_scatter(up_local.astype(jnp.bfloat16), ('ctx', 'tp'), scatter_di...  77.6 us
    reduce_scatter x1, waiting for transfers between devices, shards(): lax.psum_scatter(down_local.astype(jnp.bfloat16), ('ctx', 'tp'), scatter_...  76 us
    dot_general x6, matrix products, head_backward(): jnp.einsum('qd,kd->qk', query, keys, preferred_element_type=jnp.float32)  53 us
    all_to_all x1, blocking collectives, shards(): lax.all_to_all(rows_grad.astype(jnp.bfloat16), 'fsdp', split_axis=0, conc...  51.3 us
    all_gather x1, waiting for transfers between devices, dense_weights(): lax.all_gather(qkv_weight, 'fsdp', axis=1, tiled=True)  45.3 us
    dot_general x1, matrix products, shards(): jnp.einsum('sekd,edf->sekf', arrived, up_full, preferred_element_type=jnp...  43.7 us
  transfers between devices with their start and end apart: 24, of which 15 were waited for; matrix products, arithmetic and copies ran while one was open for 17% of the time, Pallas kernels for 0%

profile of v1, /device:TPU:0, one launch (start us, length us, event | category | flops | bytes accessed | tf_op | source)
XLA Modules:
  0.0 1489.1 jit_solution(15589165574793478174)
XLA Ops:
  14.4 45.3 %all-gather.12.cloned.1.call-done = bf16[3,768,384]{2,1,0:T(8,128)(2,1)} async-done(((bf16[3,96,384]{2,1,0:T(8,128)(2,1)}), bf16[3,768,384]{2,1,0:T(8,128)(2,1)}) %all-gather.12.cloned.1.call-update) | async-done | bytes 1769488 | tf_op jit(solution)/shard_map/all_gather | solution.py:51
  79.7 13.3 all-gather.22.cloned.1.call-done
  96.1 26.3 %all-gather.24.cloned.1.call-done = bf16[1,2048,384]{1,2,0:T(8,128)(2,1)} async-done(((bf16[1,1024,384]{1,2,0:T(8,128)(2,1)}), bf16[1,2048,384]{1,2,0:T(8,128)(2,1)}) %all-gather.24.cloned.1.call-update) | async-done | bytes 1572880 | tf_op jit(solution)/shard_map/all_gather | solution.py:143
  130.0 82.4 %while.28 = (s32[]{:T(128)}, bf16[6,1280,64]{1,2,0:T(8,128)(2,1)}, f32[6,1280]{1,0:T(8,128)}, bf16[6,1280,64]{2,1,0:T(8,128)(2,1)}, bf16[6,2304,64]{2,1,0:T(8,12...) while((s32[]{:T(128)}, bf16[6,1280,64]{1,2,0:T(8,128)(2,1)}, ...), condition=%wide.region_5.6_spmd.clone, body=%wide.region_2.5_spmd.clone.sunk | while | flops 799292160 | bytes 37163152 | solution.py:151
  130.0 6.9 fusion.199
  143.7 6.9 fusion.199
  221.1 18.6 %all-reduce.5.cloned.1.call-done = bf16[1280,768]{1,0:T(8,128)(2,1)} async-done(((bf16[1280,768]{1,0:T(8,128)(2,1)}), bf16[1280,768]{1,0:T(8,128)(2,1)}) %all-reduce.5.cloned.1.call-update) | async-done | bytes 1966096 | tf_op jit(solution)/shard_map/psum | solution.py:69
  273.9 26.3 %all-to-all-done.1 = bf16[8,2,80,768]{3,2,1,0:T(8,128)(2,1)} async-done(((bf16[8,2,80,768]{3,2,1,0:T(8,128)(2,1)}), bf16[8,2,80,768]{3,2,1,0:T(8,128)(2,1)}, u32[]{:S(2)}, u32[]{:S(2)}) %all-to-all-start.1) | async-done | bytes 1966112 | tf_op jit(solution)/shard_map/all_to_all | solution.py:184
  306.3 43.7 %fusion.66 = (bf16[8,2,80,3072]{3,2,0,1:T(8,128)(2,1)}, f32[8,2,80,3072]{3,2,0,1:T(8,128)}, f32[2,8,80,3072]{3,2,1,0:T(8,128)}) fusion(f32[2,3072]{1,0:T(2,128)S(1)} %convert_element_type.197, bf16[2,768,3072]{2,1,0:T(8,128)(2,1)} %all-gather.14.cloned.1.call-done, bf16[8,2,80,768]{3,2,1,0:T(8,128)(2,1)} %all-to-all-done.1), kind=kOutput, calls=%fused_computation.82 | convolution fusion | flops 6299320320 | bytes 50749440 | tf_op jit(solution)/shard_map/sekd,edf->sekf/dot_general | solution.py:187
  350.0 13.3 fusion.110
  363.9 23.0 %fusion.167 = (bf16[2,3072]{1,0:T(2,128)(2,1)}, bf16[8,2,80,3072]{3,2,0,1:T(8,128)(2,1)}) fusion(f32[8,2,80,3072]{3,2,0,1:T(8,128)} %get-tuple-element.291, bf16[2,3072,768]{2,1,0:T(8,128)(2,1)} %all-gather.16.cloned.1.call-done, f32[8,2,80]{2,0,1:T(8,128)S(1)} %divide_bitcast_fusion, bf16[8,2,80,768]{3,2,1,0:T(8,128)(2,1)S(1)} %all-to-all-done.3, ...), kind=kOutput, calls=%fused_computation.234 | convolution fusion | flops 6105655296 | bytes 50766848 | tf_op jit(solution)/shard_map/sekd,efd->sekf/dot_general | solution.py:227
  386.9 11.4 fusion.118
  398.4 51.3 %all_to_all.26 = bf16[8,2,80,768]{3,2,1,0:T(8,128)(2,1)S(1)} all-to-all(bf16[8,2,80,768]{3,2,1,0:T(8,128)(2,1)S(1)} %copy.91), channel_id=1, replica_groups=mesh['fsdp'=8,'ctx'=2,'tp'=2] {'fsdp'}, dimensions={0} | all-to-all | bytes 3932160 | tf_op jit(solution)/shard_map/all_to_all | solution.py:238
  452.5 9.1 all-gather.20.cloned.1.call-done
  475.4 139.5 %while.29 = (s32[]{:T(128)}, bf16[6,1280,64]{1,2,0:T(8,128)(2,1)}, bf16[6,2304,64]{1,2,0:T(8,128)(2,1)}, bf16[6,2304,64]{1,2,0:T(8,128)(2,1)}, bf16[6,1280,64]{2...) while((s32[]{:T(128)}, bf16[6,1280,64]{1,2,0:T(8,128)(2,1)}, ...), condition=%wide.region_17.18_spmd.clone, body=%wide.region_15.17_spmd.clone.sunk | while | flops 1934850816 | bytes 107280608 | solution.py:282
  479.1 8.8 multiply_reduce_fusion.3
  502.3 8.8 multiply_reduce_fusion.3
  525.5 8.8 multiply_reduce_fusion.3
  548.7 8.8 multiply_reduce_fusion.3
  571.9 8.8 multiply_reduce_fusion.3
  595.0 8.8 multiply_reduce_fusion.3
  631.4 14.0 reduce-scatter.23.cloned.1.call-done
  645.4 29.0 %reduce-scatter.21.cloned.1.call-done = bf16[1024,384]{1,0:T(8,128)(2,1)} async-done(((bf16[2048,384]{1,0:T(8,128)(2,1)}), bf16[1024,384]{1,0:T(8,128)(2,1)}) %reduce-scatter.21.cloned.1.call-update) | async-done | bytes 786448 | tf_op jit(solution)/shard_map/reduce_scatter | solution.py:289
  690.9 10.9 all-reduce.7.cloned.1.call-done
  719.5 13.0 bitcast_convert_fusion.1
  732.6 13.1 bitcast_convert_fusion
  763.6 117.2 %reduce-scatter.31.cloned.1.call-done = f32[48,2]{1,0:T(8,128)} async-done(((f32[768,2]{1,0:T(8,128)}), f32[48,2]{1,0:T(8,128)}) %reduce-scatter.31.cloned.1.call-update) | async-done | bytes 400
  882.1 125.5 %reduce-scatter.33.cloned.1.call-done = f32[48,2]{1,0:T(8,128)} async-done(((f32[768,2]{1,0:T(8,128)}), f32[48,2]{1,0:T(8,128)}) %reduce-scatter.33.cloned.1.call-update) | async-done | bytes 400
  1009.0 182.4 %all-reduce.9.cloned.1.call-done = f32[3,768,384]{2,0,1:T(4,128)} async-done(((f32[3,768,384]{2,0,1:T(4,128)}), f32[3,768,384]{2,0,1:T(4,128)}) %all-reduce.9.cloned.1.call-update) | async-done | bytes 3538960
  1193.0 77.6 %reduce-scatter.27.cloned.1.call-done = bf16[2,192,3072]{2,1,0:T(8,128)(2,1)} async-done(((bf16[2,768,3072]{2,1,0:T(8,128)(2,1)}), bf16[2,192,3072]{2,1,0:T(8,128)(2,1)}) %reduce-scatter.27.cloned.1.call-update) | async-done | bytes 2359312 | tf_op jit(solution)/shard_map/reduce_scatter | solution.py:251
  1275.1 76.0 %reduce-scatter.29.cloned.1.call-done = bf16[2,768,768]{2,1,0:T(8,128)(2,1)} async-done(((bf16[2,3072,768]{2,1,0:T(8,128)(2,1)}), bf16[2,768,768]{2,1,0:T(8,128)(2,1)}) %reduce-scatter.29.cloned.1.call-update) | async-done | bytes 2359312 | tf_op jit(solution)/shard_map/reduce_scatter | solution.py:254
  1355.3 126.0 %reduce-scatter.25.cloned.1.call-done = f32[384,48]{0,1:T(8,128)} async-done(((f32[384,768]{0,1:T(8,128)}), f32[384,48]{0,1:T(8,128)}) %reduce-scatter.25.cloned.1.call-update) | async-done | bytes 73744 | tf_op jit(solution)/shard_map/reduce_scatter | solution.py:314
  (353 shorter events, 337.8 us)
Async XLA Ops:
  8.0 51.7 %copy-start = (bf16[1,1,1280,768]{3,2,1,0:T(8,128)(2,1)S(1)}, bf16[1,1,1280,768]{3,2,1,0:T(8,128)(2,1)}, u32[]{:S(2)}) copy-start(bf16[1,1,1280,768]{3,2,1,0:T(8,128)(2,1)} %param.16) | copy-start | bytes 5898244
  8.0 51.7 %all-gather.12.cloned.1.call-start = ((), (), s32[]{:S(2)}) async-start(), calls=%async_computation.15 | async-start | bytes 1990656 | tf_op jit(solution)/shard_map/all_gather | solution.py:51
  8.8 84.2 %all-gather.22.cloned.1.call-start = ((), (), s32[]{:S(2)}) async-start(), calls=%async_computation.27 | async-start | bytes 2359296 | tf_op jit(solution)/shard_map/all_gather | solution.py:142
  10.2 53.8 %copy-start.27 = (f32[768]{0:T(1024)}, f32[768]{0:T(1024)S(1)}, u32[]{:S(2)}) copy-start(f32[768]{0:T(1024)S(1)} %get-tuple-element.307) | copy-start | bytes 9220
  10.2 53.8 %copy-start.39 = (f32[768]{0:T(1024)}, f32[768]{0:T(1024)S(1)}, u32[]{:S(2)}) copy-start(f32[768]{0:T(1024)S(1)} %get-tuple-element.233) | copy-start | bytes 9220
  12.1 52.0 %copy-start.20 = (f32[1280]{0:T(1024)}, f32[1280]{0:T(1024)S(1)}, u32[]{:S(2)}) copy-start(f32[1280]{0:T(1024)S(1)} %broadcast_multiply_fusion.5) | copy-start | bytes 15364
  14.4 49.7 %copy-start.22 = (f32[1280]{0:T(1024)}, f32[1280]{0:T(1024)S(1)}, u32[]{:S(2)}) copy-start(f32[1280]{0:T(1024)S(1)} %add_rsqrt_fusion.1) | copy-start | bytes 15364
  67.1 55.3 %all-gather.24.cloned.1.call-start = ((), (), s32[]{:S(2)}) async-start(), calls=%async_computation.28 | async-start | bytes 2359296 | tf_op jit(solution)/shard_map/all_gather | solution.py:143
  68.7 143.7 %all-to-all-start = ((bf16[8,384,96]{1,2,0:T(8,128)(2,1)}), bf16[8,384,96]{1,2,0:T(8,128)(2,1)}, u32[]{:S(2)}, u32[]{:S(2)}) async-start(bf16[8,384,96]{1,2,0:T(8,128)(2,1)} %stack.16), calls=%async_computation | async-start | bytes 1179648 | tf_op jit(solution)/shard_map/all_to_all | solution.py:16
  72.9 166.8 %all-reduce.5.cloned.1.call-start = ((), (), s32[]{:S(2)}) async-start(), calls=%async_computation.16 | async-start | bytes 3932160 | tf_op jit(solution)/shard_map/psum | solution.py:69
  218.0 88.3 %all-gather.14.cloned.1.call-start = ((), (), s32[]{:S(2)}) async-start(), calls=%async_computation.17 | async-start | bytes 11796480 | tf_op jit(solution)/shard_map/all_gather | solution.py:56
  218.6 131.4 %all-gather.16.cloned.1.call-start = ((), (), s32[]{:S(2)}) async-start(), calls=%async_computation.18 | async-start | bytes 11796480 | tf_op jit(solution)/shard_map/all_gather | solution.py:57
  221.1 49.8 %copy-start.41 = (s32[640]{0:T(1024)}, s32[640]{0:T(1024)S(1)}, u32[]{:S(2)}) copy-start(s32[640]{0:T(1024)S(1)} %multiply_add_fusion) | copy-start | bytes 7684
  248.6 51.6 %all-to-all-start.1 = ((bf16[8,2,80,768]{3,2,1,0:T(8,128)(2,1)}), bf16[8,2,80,768]{3,2,1,0:T(8,128)(2,1)}, u32[]{:S(2)}, u32[]{:S(2)}) async-start(bf16[8,2,80,768]{3,2,1,0:T(8,128)(2,1)} %bitcast.384), calls=%async_computation.1 | async-start | bytes 3932160 | tf_op jit(solution)/shard_map/all_to_all | solution.py:184
  300.2 49.7 %all-to-all-start.3 = ((bf16[8,2,80,768]{3,2,1,0:T(8,128)(2,1)}), bf16[8,2,80,768]{3,2,1,0:T(8,128)(2,1)S(1)}, u32[]{:S(2)}, u32[]{:S(2)}) async-start(bf16[8,2,80,768]{3,2,1,0:T(8,128)(2,1)} %bitcast.383), calls=%async_computation.3 | async-start | bytes 3932160 | tf_op jit(solution)/shard_map/all_to_all | solution.py:221
  303.9 157.8 %all-gather.20.cloned.1.call-start = ((), (), s32[]{:S(2)}) async-start(), calls=%async_computation.20 | async-start | bytes 2949120 | tf_op jit(solution)/shard_map/all_gather | solution.py:65
  306.3 57.6 %copy-start.31 = (f32[8,2,80]{2,0,1:T(8,128)}, f32[8,2,80]{2,0,1:T(8,128)S(1)}, u32[]{:S(2)}) copy-start(f32[8,2,80]{2,0,1:T(8,128)S(1)} %divide_bitcast_fusion) | copy-start | bytes 15364
  398.3 51.4 %copy-start.42 = (s32[640]{0:T(1024)S(1)}, s32[640]{0:T(1024)}, u32[]{:S(2)}) copy-start(s32[640]{0:T(1024)} %copy-done.41) | copy-start | bytes 7684
  452.4 193.0 %reduce-scatter.23.cloned.1.call-start = ((), (), s32[]{:S(2)}) async-start(), calls=%async_computation.22 | async-start | bytes 2359296 | tf_op jit(solution)/shard_map/reduce_scatter | solution.py:292
  618.0 56.5 %reduce-scatter.21.cloned.1.call-start = ((), (), s32[]{:S(2)}) async-start(), calls=%async_computation.21 | async-start | bytes 2359296 | tf_op jit(solution)/shard_map/reduce_scatter | solution.py:289
  622.7 63.6 %all-to-all-start.2 = ((bf16[8,2,80,768]{3,2,1,0:T(8,128)(2,1)}), bf16[8,2,80,768]{3,2,1,0:T(8,128)(2,1)}, u32[]{:S(2)}, u32[]{:S(2)}) async-start(bf16[8,2,80,768]{3,2,1,0:T(8,128)(2,1)} %copy.89), calls=%async_computation.2 | async-start | bytes 3932160 | tf_op jit(solution)/shard_map/all_to_all | solution.py:195
  628.5 73.3 %all-reduce.7.cloned.1.call-start = ((), (), s32[]{:S(2)}) async-start(), calls=%async_computation.23 | async-start | bytes 3932160 | tf_op jit(solution)/shard_map/psum | solution.py:69
  680.6 72.0 %reduce-scatter.37.cloned.1.call-start = ((), (), s32[]{:S(2)}) async-start(), calls=%async_computation.32 | async-start | bytes 245760
  682.0 72.1 %reduce-scatter.39.cloned.1.call-start = ((), (), s32[]{:S(2)}) async-start(), calls=%async_computation.33 | async-start | bytes 245760
  685.0 70.6 %reduce-scatter.35.cloned.1.call-start = ((), (), s32[]{:S(2)}) async-start(), calls=%async_computation.31 | async-start | bytes 983040
  686.3 71.0 %all-gather.18.cloned.1.call-start = ((), (), s32[]{:S(2)}) async-start(), calls=%async_computation.19 | async-start | bytes 2949120 | tf_op jit(solution)/shard_map/all_gather | solution.py:65
  690.8 190.0 %reduce-scatter.31.cloned.1.call-start = ((), (), s32[]{:S(2)}) async-start(), calls=%async_computation.29 | async-start | bytes 417792
  706.2 301.4 %reduce-scatter.33.cloned.1.call-start = ((), (), s32[]{:S(2)}) async-start(), calls=%async_computation.30 | async-start | bytes 417792
  707.2 484.1 %all-reduce.9.cloned.1.call-start = ((), (), s32[]{:S(2)}) async-start(), calls=%async_computation.34 | async-start | bytes 9437184
  719.5 551.2 %reduce-scatter.27.cloned.1.call-start = ((), (), s32[]{:S(2)}) async-start(), calls=%async_computation.25 | async-start | bytes 11796480 | tf_op jit(solution)/shard_map/reduce_scatter | solution.py:251
  732.5 618.6 %reduce-scatter.29.cloned.1.call-start = ((), (), s32[]{:S(2)}) async-start(), calls=%async_computation.26 | async-start | bytes 11796480 | tf_op jit(solution)/shard_map/reduce_scatter | solution.py:254
  745.8 735.5 %reduce-scatter.25.cloned.1.call-start = ((), (), s32[]{:S(2)}) async-start(), calls=%async_computation.24 | async-start | bytes 1253376 | tf_op jit(solution)/shard_map/reduce_scatter | solution.py:314
  (54 other events, 366.0 us)
Sparse Core Ops, SparseCore 0:
  11.0 48.6 all-gather.11
  67.2 25.7 all-gather.21
  95.1 27.1 all-gather.23
  218.2 21.4 all-reduce.4
  452.5 9.0 all-gather.19
  618.1 27.3 reduce-scatter.22
  648.3 26.1 reduce-scatter.20
  680.7 21.0 all-reduce.6
  703.4 11.5 all-gather.17
Sparse Core Ops, SparseCore 1:
  220.1 64.2 all-gather.13
  285.7 64.1 all-gather.15
  684.1 19.7 reduce-scatter.36
  706.4 20.7 reduce-scatter.38
  729.7 23.1 reduce-scatter.34
  757.5 123.2 reduce-scatter.30
  885.3 122.2 reduce-scatter.32
  1013.8 177.5 all-reduce.8
  1193.8 76.8 reduce-scatter.26
  1273.3 77.8 reduce-scatter.28
  1356.3 124.9 reduce-scatter.24
